TPU v7x, 32 devices: a whole 2x2x4 slice. The times are simulated.
32 devices in a mesh: sec: 4 (over x, core), row: 8 (over z, y).
Axes of the slice: x: 2, y: 2, z: 4, core: 2. Of those that a mesh axis runs over, the one named last changes fastest.
Arguments:
- factor: float32 [4, 2048, 8192], P(None, 'row', 'sec'), may hold values from -0.0625 to 0.0625
- inverse_blocks: float32 [4, 2048, 2048], P('sec', 'row'), may hold values from -4 to 4, as said below
- right_side: float32 [4, 2048, 384], P('sec', 'row'), may hold values from -6 to 6
Outputs:
- solution: float32 [4, 2048, 384], P('sec', 'row')
Inputs may be any that keep to these rules, and one draw needn't show every extreme that they name: `inverse_blocks`: each block is nonsingular; it stands for the inverse of the factor's diagonal block of that section.
All inputs are finite; a program needn't handle non-finite values.
Results may differ from a plain program's by a relative error of at most 0.0001.
Values sent between devices are 32-bit elements; how exact they have to be, the bound alone decides.
A program may use at most 64 MiB of HBM per device.

v0:
```python
import jax
import jax.numpy as jnp
from jax import lax
from jax.sharding import PartitionSpec as P

MICRO = 3
WIDTH = 128


highest = lax.Precision.HIGHEST


def passed_along(block, axis, distance):
    devices = range(lax.axis_size(axis))
    route = [(i - distance, i) for i in devices if i - distance in devices]
    return lax.ppermute(block, axis, route)


def shards(factor, inverse_blocks, right_side):
    sections = lax.axis_size("sec")
    segment = lax.axis_index("sec")
    local_rows = factor.shape[1]
    block_cols = factor.shape[2]
    width = WIDTH
    own_inverse = inverse_blocks[0]
    panel_rows = factor.reshape(sections * local_rows, block_cols)

    def fold_update(carry, piece):
        return carry + jnp.dot(panel_rows, piece, precision=highest)

    def advance(tick_index, state):
        carried, head, solution = state
        group = tick_index - segment
        valid = jnp.logical_and(group >= 0, group < MICRO)
        clipped = jnp.clip(group, 0, MICRO - 1)
        start_col = clipped * width
        own_rhs = lax.dynamic_slice_in_dim(right_side[0], start_col, width, 1)
        own_sum = head
        residual = own_rhs - own_sum
        full_residual = lax.all_gather(residual, "row", axis=0, tiled=True)
        own_result = jnp.dot(own_inverse, full_residual, precision=highest)
        updated = lax.dynamic_update_slice_in_dim(solution, own_result, start_col, 1)
        solution = jnp.where(valid, updated, solution)
        flat_in = carried.reshape(sections * local_rows, width)
        outgoing = fold_update(flat_in, lax.all_gather(own_result, "row", axis=0, tiled=True))
        outgoing = outgoing.reshape(sections, local_rows, width)
        following = jnp.minimum(segment + 1, sections - 1)
        next_sum = lax.dynamic_index_in_dim(outgoing, following, 0, keepdims=False)
        head = passed_along(next_sum, "sec", 1)
        carried = passed_along(outgoing, "sec", 1)
        return (carried, head, solution)

    initial = (
        jnp.zeros((sections, local_rows, width), jnp.float32),
        jnp.zeros((local_rows, width), jnp.float32),
        jnp.zeros(right_side.shape[1:], jnp.float32),
    )
    final = lax.fori_loop(0, sections + MICRO - 1, advance, initial)
    return final[2][None]


def solution(mesh):
    return jax.shard_map(
        shards,
        mesh=mesh,
        in_specs=(P(None, "row", "sec"), P("sec", "row", None), P("sec", "row", None)),
        out_specs=P("sec", "row", None),
        check_vma=False,
    )
```

profile of v0, /device:TPU:3, one launch (start us, length us, event | category | flops | bytes accessed | tf_op | source)
XLA Modules:
  0.0 659.4 jit_solution(2073231575732520902)
XLA Ops:
  6.7 645.1 %while.19 = (s32[]{:T(128)}, f32[4,256,128]{1,0,2:T(4,128)S(1)}, f32[256,128]{0,1:T(8,128)S(1)}, f32[256,384]{1,0:T(8,128)S(1)}, s32[]{:T(128)}, /*index=5*/f32[...) while((s32[]{:T(128)}, f32[4,256,128]{1,0,2:T(4,128)S(1)}, ...), condition=%wide.region_1.2_spmd, body=%wide.region_0.1_spmd.sunk | while | flops 4026728448 | bytes 28311972 | solution.py:58
  6.7 0.9 constant_dynamic-slice_fusion.7
  7.8 0.7 bitcast_subtract_fusion.2
  8.7 41.0 %all-gather.3.cloned.1.call-done = f32[2048,128]{0,1:T(8,128)} async-done(((f32[256,128]{0,1:T(8,128)}), f32[2048,128]{0,1:T(8,128)}) %all-gather.3.cloned.1.call-update) | async-done | bytes 1048592 | tf_op jit(solution)/shard_map/while/body/eval_jaxpr/all_gather | solution.py:40
  49.7 4.8 broadcast_select_fusion.2
  54.6 38.5 %all-gather.5.cloned.1.call-done = f32[2048,128]{0,1:T(8,128)} async-done(((f32[256,128]{0,1:T(8,128)}), f32[2048,128]{0,1:T(8,128)}) %all-gather.5.cloned.1.call-update) | async-done | bytes 1048592 | tf_op jit(solution)/shard_map/while/body/eval_jaxpr/all_gather | solution.py:45
  93.1 11.4 %fusion.14 = f32[1024,128]{0,1:T(8,128)S(1)} fusion(f32[1024,128]{0,1:T(8,128)S(1)} %bitcast.43, f32[2048,128]{0,1:T(8,128)} %all-gather.5.cloned.1.call-done, f32[1024,2048]{1,0:T(8,128)} %get-tuple-element.330), kind=kOutput, calls=%fused_computation.1.clone.1 | convolution fusion | flops 3221356544 | bytes 10485760 | tf_op jit(solution)/shard_map/while/body/eval_jaxpr/dot_general | solution.py:29
  104.5 0.2 reshape.28
  104.7 1.3 collective-permute-start
  106.2 1.3 collective-permute-start.1
  107.6 3.2 collective-permute-done.1
  110.8 0.9 constant_dynamic-slice_fusion.7
  111.9 0.7 bitcast_subtract_fusion.2
  112.8 45.2 %all-gather.3.cloned.1.call-done = f32[2048,128]{0,1:T(8,128)} async-done(((f32[256,128]{0,1:T(8,128)}), f32[2048,128]{0,1:T(8,128)}) %all-gather.3.cloned.1.call-update) | async-done | bytes 1048592 | tf_op jit(solution)/shard_map/while/body/eval_jaxpr/all_gather | solution.py:40
  157.9 4.8 broadcast_select_fusion.2
  162.8 38.5 %all-gather.5.cloned.1.call-done = f32[2048,128]{0,1:T(8,128)} async-done(((f32[256,128]{0,1:T(8,128)}), f32[2048,128]{0,1:T(8,128)}) %all-gather.5.cloned.1.call-update) | async-done | bytes 1048592 | tf_op jit(solution)/shard_map/while/body/eval_jaxpr/all_gather | solution.py:45
  201.3 11.4 %fusion.14 = f32[1024,128]{0,1:T(8,128)S(1)} fusion(f32[1024,128]{0,1:T(8,128)S(1)} %bitcast.43, f32[2048,128]{0,1:T(8,128)} %all-gather.5.cloned.1.call-done, f32[1024,2048]{1,0:T(8,128)} %get-tuple-element.330), kind=kOutput, calls=%fused_computation.1.clone.1 | convolution fusion | flops 3221356544 | bytes 10485760 | tf_op jit(solution)/shard_map/while/body/eval_jaxpr/dot_general | solution.py:29
  212.7 0.2 reshape.28
  213.0 1.3 collective-permute-start
  214.3 0.1 constant_dynamic-slice_fusion.8
  214.4 1.3 collective-permute-start.1
  215.8 3.2 collective-permute-done.1
  219.1 0.9 constant_dynamic-slice_fusion.7
  220.1 0.7 bitcast_subtract_fusion.2
  221.0 44.9 %all-gather.3.cloned.1.call-done = f32[2048,128]{0,1:T(8,128)} async-done(((f32[256,128]{0,1:T(8,128)}), f32[2048,128]{0,1:T(8,128)}) %all-gather.3.cloned.1.call-update) | async-done | bytes 1048592 | tf_op jit(solution)/shard_map/while/body/eval_jaxpr/all_gather | solution.py:40
  265.9 4.8 broadcast_select_fusion.2
  270.8 38.5 %all-gather.5.cloned.1.call-done = f32[2048,128]{0,1:T(8,128)} async-done(((f32[256,128]{0,1:T(8,128)}), f32[2048,128]{0,1:T(8,128)}) %all-gather.5.cloned.1.call-update) | async-done | bytes 1048592 | tf_op jit(solution)/shard_map/while/body/eval_jaxpr/all_gather | solution.py:45
  309.2 11.4 %fusion.14 = f32[1024,128]{0,1:T(8,128)S(1)} fusion(f32[1024,128]{0,1:T(8,128)S(1)} %bitcast.43, f32[2048,128]{0,1:T(8,128)} %all-gather.5.cloned.1.call-done, f32[1024,2048]{1,0:T(8,128)} %get-tuple-element.330), kind=kOutput, calls=%fused_computation.1.clone.1 | convolution fusion | flops 3221356544 | bytes 10485760 | tf_op jit(solution)/shard_map/while/body/eval_jaxpr/dot_general | solution.py:29
  320.6 0.2 reshape.28
  320.9 1.3 collective-permute-start
  322.2 0.1 constant_dynamic-slice_fusion.8
  322.3 1.3 collective-permute-start.1
  323.8 3.2 collective-permute-done.1
  327.0 0.9 constant_dynamic-slice_fusion.7
  328.0 0.7 bitcast_subtract_fusion.2
  328.9 45.2 %all-gather.3.cloned.1.call-done = f32[2048,128]{0,1:T(8,128)} async-done(((f32[256,128]{0,1:T(8,128)}), f32[2048,128]{0,1:T(8,128)}) %all-gather.3.cloned.1.call-update) | async-done | bytes 1048592 | tf_op jit(solution)/shard_map/while/body/eval_jaxpr/all_gather | solution.py:40
  374.1 4.8 broadcast_select_fusion.2
  379.0 38.5 %all-gather.5.cloned.1.call-done = f32[2048,128]{0,1:T(8,128)} async-done(((f32[256,128]{0,1:T(8,128)}), f32[2048,128]{0,1:T(8,128)}) %all-gather.5.cloned.1.call-update) | async-done | bytes 1048592 | tf_op jit(solution)/shard_map/while/body/eval_jaxpr/all_gather | solution.py:45
  417.5 11.4 %fusion.14 = f32[1024,128]{0,1:T(8,128)S(1)} fusion(f32[1024,128]{0,1:T(8,128)S(1)} %bitcast.43, f32[2048,128]{0,1:T(8,128)} %all-gather.5.cloned.1.call-done, f32[1024,2048]{1,0:T(8,128)} %get-tuple-element.330), kind=kOutput, calls=%fused_computation.1.clone.1 | convolution fusion | flops 3221356544 | bytes 10485760 | tf_op jit(solution)/shard_map/while/body/eval_jaxpr/dot_general | solution.py:29
  428.9 0.2 reshape.28
  429.2 1.3 collective-permute-start
  430.6 1.3 collective-permute-start.1
  432.0 3.2 collective-permute-done.1
  435.3 0.9 constant_dynamic-slice_fusion.7
  436.3 0.7 bitcast_subtract_fusion.2
  437.2 45.2 %all-gather.3.cloned.1.call-done = f32[2048,128]{0,1:T(8,128)} async-done(((f32[256,128]{0,1:T(8,128)}), f32[2048,128]{0,1:T(8,128)}) %all-gather.3.cloned.1.call-update) | async-done | bytes 1048592 | tf_op jit(solution)/shard_map/while/body/eval_jaxpr/all_gather | solution.py:40
  482.4 4.8 broadcast_select_fusion.2
  487.3 38.5 %all-gather.5.cloned.1.call-done = f32[2048,128]{0,1:T(8,128)} async-done(((f32[256,128]{0,1:T(8,128)}), f32[2048,128]{0,1:T(8,128)}) %all-gather.5.cloned.1.call-update) | async-done | bytes 1048592 | tf_op jit(solution)/shard_map/while/body/eval_jaxpr/all_gather | solution.py:45
  525.7 11.4 %fusion.14 = f32[1024,128]{0,1:T(8,128)S(1)} fusion(f32[1024,128]{0,1:T(8,128)S(1)} %bitcast.43, f32[2048,128]{0,1:T(8,128)} %all-gather.5.cloned.1.call-done, f32[1024,2048]{1,0:T(8,128)} %get-tuple-element.330), kind=kOutput, calls=%fused_computation.1.clone.1 | convolution fusion | flops 3221356544 | bytes 10485760 | tf_op jit(solution)/shard_map/while/body/eval_jaxpr/dot_general | solution.py:29
  537.1 0.2 reshape.28
  537.4 1.3 collective-permute-start
  538.8 1.3 collective-permute-start.1
  540.3 3.2 collective-permute-done.1
  543.5 0.9 constant_dynamic-slice_fusion.7
  544.5 0.7 bitcast_subtract_fusion.2
  545.4 45.2 %all-gather.3.cloned.1.call-done = f32[2048,128]{0,1:T(8,128)} async-done(((f32[256,128]{0,1:T(8,128)}), f32[2048,128]{0,1:T(8,128)}) %all-gather.3.cloned.1.call-update) | async-done | bytes 1048592 | tf_op jit(solution)/shard_map/while/body/eval_jaxpr/all_gather | solution.py:40
  590.6 4.8 broadcast_select_fusion.2
  595.5 38.5 %all-gather.5.cloned.1.call-done = f32[2048,128]{0,1:T(8,128)} async-done(((f32[256,128]{0,1:T(8,128)}), f32[2048,128]{0,1:T(8,128)}) %all-gather.5.cloned.1.call-update) | async-done | bytes 1048592 | tf_op jit(solution)/shard_map/while/body/eval_jaxpr/all_gather | solution.py:45
  634.0 11.4 %fusion.14 = f32[1024,128]{0,1:T(8,128)S(1)} fusion(f32[1024,128]{0,1:T(8,128)S(1)} %bitcast.43, f32[2048,128]{0,1:T(8,128)} %all-gather.5.cloned.1.call-done, f32[1024,2048]{1,0:T(8,128)} %get-tuple-element.330), kind=kOutput, calls=%fused_computation.1.clone.1 | convolution fusion | flops 3221356544 | bytes 10485760 | tf_op jit(solution)/shard_map/while/body/eval_jaxpr/dot_general | solution.py:29
  645.4 0.2 reshape.28
  645.6 1.3 collective-permute-start
  647.1 1.3 collective-permute-start.1
  648.5 3.2 collective-permute-done.1
  651.8 0.7 copy-done
  (80 shorter events, 3.6 us)
Async XLA Ops:
  6.7 43.0 %all-gather.3.cloned.1.call-start = ((), (), s32[]{:S(2)}) async-start(), calls=%async_computation | async-start | bytes 1179648 | tf_op jit(solution)/shard_map/while/body/eval_jaxpr/all_gather | solution.py:40
  8.5 84.6 %all-gather.5.cloned.1.call-start = ((), (), s32[]{:S(2)}) async-start(), calls=%async_computation.1 | async-start | bytes 1179648 | tf_op jit(solution)/shard_map/while/body/eval_jaxpr/all_gather | solution.py:45
  104.7 6.1 collective-permute-start
  106.2 4.7 collective-permute-start.1
  110.8 47.1 %all-gather.3.cloned.1.call-start = ((), (), s32[]{:S(2)}) async-start(), calls=%async_computation | async-start | bytes 1179648 | tf_op jit(solution)/shard_map/while/body/eval_jaxpr/all_gather | solution.py:40
  112.6 88.7 %all-gather.5.cloned.1.call-start = ((), (), s32[]{:S(2)}) async-start(), calls=%async_computation.1 | async-start | bytes 1179648 | tf_op jit(solution)/shard_map/while/body/eval_jaxpr/all_gather | solution.py:45
  213.0 6.1 collective-permute-start
  214.4 4.7 collective-permute-start.1
  219.1 46.8 %all-gather.3.cloned.1.call-start = ((), (), s32[]{:S(2)}) async-start(), calls=%async_computation | async-start | bytes 1179648 | tf_op jit(solution)/shard_map/while/body/eval_jaxpr/all_gather | solution.py:40
  220.8 88.4 %all-gather.5.cloned.1.call-start = ((), (), s32[]{:S(2)}) async-start(), calls=%async_computation.1 | async-start | bytes 1179648 | tf_op jit(solution)/shard_map/while/body/eval_jaxpr/all_gather | solution.py:45
  320.9 6.1 collective-permute-start
  322.3 4.7 collective-permute-start.1
  327.0 47.1 %all-gather.3.cloned.1.call-start = ((), (), s32[]{:S(2)}) async-start(), calls=%async_computation | async-start | bytes 1179648 | tf_op jit(solution)/shard_map/while/body/eval_jaxpr/all_gather | solution.py:40
  328.7 88.7 %all-gather.5.cloned.1.call-start = ((), (), s32[]{:S(2)}) async-start(), calls=%async_computation.1 | async-start | bytes 1179648 | tf_op jit(solution)/shard_map/while/body/eval_jaxpr/all_gather | solution.py:45
  429.2 6.1 collective-permute-start
  430.6 4.7 collective-permute-start.1
  435.3 47.1 %all-gather.3.cloned.1.call-start = ((), (), s32[]{:S(2)}) async-start(), calls=%async_computation | async-start | bytes 1179648 | tf_op jit(solution)/shard_map/while/body/eval_jaxpr/all_gather | solution.py:40
  437.0 88.7 %all-gather.5.cloned.1.call-start = ((), (), s32[]{:S(2)}) async-start(), calls=%async_computation.1 | async-start | bytes 1179648 | tf_op jit(solution)/shard_map/while/body/eval_jaxpr/all_gather | solution.py:45
  537.4 6.1 collective-permute-start
  538.8 4.7 collective-permute-start.1
  543.5 47.1 %all-gather.3.cloned.1.call-start = ((), (), s32[]{:S(2)}) async-start(), calls=%async_computation | async-start | bytes 1179648 | tf_op jit(solution)/shard_map/while/body/eval_jaxpr/all_gather | solution.py:40
  545.2 88.7 %all-gather.5.cloned.1.call-start = ((), (), s32[]{:S(2)}) async-start(), calls=%async_computation.1 | async-start | bytes 1179648 | tf_op jit(solution)/shard_map/while/body/eval_jaxpr/all_gather | solution.py:45
  645.6 6.1 collective-permute-start
  647.1 4.7 collective-permute-start.1
  651.8 0.7 copy-start
Sparse Core Ops, SparseCore 0:
  9.5 40.1 all-gather.2
  54.6 38.3 all-gather.4
  113.7 44.1 all-gather.2
  162.9 38.4 all-gather.4
  221.6 44.1 all-gather.2
  270.8 38.3 all-gather.4
  329.9 44.1 all-gather.2
  379.0 38.4 all-gather.4
  438.1 44.1 all-gather.2
  487.3 38.4 all-gather.4
  546.4 44.1 all-gather.2
  595.5 38.4 all-gather.4
where the time goes:
time: 666 us; the launch traced here: 659 us
  waiting for transfers between devices  517 us (78%)
  matrix products  97.1 us (15%)
  starting transfers between devices  15.8 us (2%)
  between operations  13.4 us (2%)
  local copies, waits for them, and re-layouts  11.1 us (2%)
    all_gather x6, waiting for transfers between devices, advance(): full_residual = lax.all_gather(residual, 'row', axis=0, tiled=True)  267 us
    all_gather x6, waiting for transfers between devices, advance(): lax.all_gather(own_result, 'row', axis=0, tiled=True)  231 us
    dot_general x6, matrix products, fold_update(): return carry + jnp.dot(panel_rows, piece, precision=highest)  68.4 us
    dot_general x6, matrix products, advance(): own_result = jnp.dot(own_inverse, full_residual, precision=highest)  28.7 us
    ppermute x12, waiting for transfers between devices, passed_along(): return lax.ppermute(block, axis, route)  19.5 us
    ppermute x12, starting transfers between devices, passed_along(): return lax.ppermute(block, axis, route)  15.5 us
  transfers between devices with their start and end apart: 24, of which 18 were waited for; matrix products, arithmetic and copies ran while one was open for 0% of the time, Pallas kernels for 0%

commit v1 on v0

v1 whole, which is shorter than its diff:
```python
import functools

import jax
import jax.numpy as jnp
from jax import lax
from jax.experimental import pallas as pl
from jax.experimental.pallas import tpu as pltpu
from jax.sharding import PartitionSpec as P

MESH = pl.DeviceIdType.MESH
WIDTH = 128


def split(value):
    high = value.astype(jnp.bfloat16)
    low = (value - high.astype(jnp.float32)).astype(jnp.bfloat16)
    return high, low


def kernel(
    sections, lines, columns, micro,
    factor, inverse, rhs, out,
    staged, panels, residuals, solved, operand, product, arrived, leaving,
    load_sem, send_sem, recv_sem, part_send, part_recv,
):
    width = WIDTH
    rows = rhs.shape[0]
    group = lines * columns
    sec = lax.axis_index("sec")
    me = lax.axis_index("row")
    z, y = me // columns, me % columns
    z_steps = [s for d in range(1, lines) for s in ([d] if 2 * d == lines else [d, lines - d]) if 2 * d <= lines]
    z_peers = [lax.rem(z + s, lines) * columns + y for s in z_steps]
    y_peers = [z * columns + lax.rem(y + s, columns) for s in range(1, columns)]
    lines_of = [lax.rem(z + s, lines) for s in z_steps]

    def load(slot, source):
        return pltpu.make_async_copy(source, staged.at[slot], load_sem.at[slot])

    load(0, inverse).start()

    def start_load(i, carry):
        load(i, factor.at[i]).start()
        return carry

    lax.fori_loop(sec + 1, sections, start_load, 0)

    barrier = pltpu.get_barrier_semaphore()
    for peer in z_peers + y_peers:
        pl.semaphore_signal(barrier, inc=1, device_id=(sec, peer), device_id_type=MESH)
    for s in range(1, sections):
        pl.semaphore_signal(barrier, inc=1, device_id=(lax.rem(sec + s, sections), me), device_id_type=MESH)
    pl.semaphore_wait(barrier, len(z_peers) + len(y_peers) + sections - 1)

    def prepare(slot, carry):
        load(slot, factor.at[slot]).wait()
        step = 64 if rows % 64 == 0 else rows

        def part(j, carry):
            at = pl.multiple_of(j * step, step)
            high, low = split(staged[slot, pl.ds(at, step), :])
            panels[slot, pl.ds(at, step), :] = high
            panels[slot, pl.ds(pl.multiple_of(rows + at, step), step), :] = low
            return carry

        return lax.fori_loop(0, rows // step, part, carry)

    def place(source):
        return pl.ds(pl.multiple_of(source * rows, rows), rows)

    def copy_of(buffer, kind, c, source, number, peer):
        return pltpu.make_async_remote_copy(
            src_ref=buffer.at[c, place(source), :],
            dst_ref=buffer.at[c, place(source), :],
            send_sem=send_sem.at[kind, c, number],
            recv_sem=recv_sem.at[kind, c, source],
            device_id=(sec, peer),
            device_id_type=MESH,
        )

    def spread(buffer, kind, c):
        for number, peer in enumerate(z_peers + y_peers):
            copy_of(buffer, kind, c, me, number, peer).start()

    def digest(buffer, c, source):
        high, low = split(buffer[c, place(source), :])
        operand[place(source), pl.ds(0, width)] = high
        operand[place(source), pl.ds(width, width)] = low

    def relay(buffer, kind, c):
        number = len(z_peers) + len(y_peers)
        for peer in z_peers:
            copy_of(buffer, kind, c, peer, 0, me).wait_recv()
            for target in y_peers:
                copy_of(buffer, kind, c, peer, number, target).start()
                number += 1
            digest(buffer, c, peer)

    def finish(buffer, kind, c):
        digest(buffer, c, me)
        for s in range(1, columns):
            column = lax.rem(y + s, columns)
            for line in [z] + lines_of:
                source = line * columns + column
                copy_of(buffer, kind, c, source, 0, me).wait_recv()
                digest(buffer, c, source)

    def multiply(slot):
        product[...] = jnp.dot(panels[slot], operand[...], preferred_element_type=jnp.float32)
        upper = product[pl.ds(0, rows), pl.ds(0, width)] + product[pl.ds(0, rows), pl.ds(width, width)]
        lower = product[pl.ds(rows, rows), pl.ds(0, width)] + product[pl.ds(rows, rows), pl.ds(width, width)]
        return upper + lower

    def part_copy(source, target, c):
        return pltpu.make_async_remote_copy(
            src_ref=leaving.at[target, c],
            dst_ref=arrived.at[source, c],
            send_sem=part_send.at[target, c],
            recv_sem=part_recv.at[source, c],
            device_id=(target, me),
            device_id_type=MESH,
        )

    def begin(c):
        cols = pl.ds(pl.multiple_of(c * width, width), width)
        residuals[c, place(me), :] = rhs[:, cols]

        def subtract(k, carry):
            part_copy(k, sec, c).wait_recv()
            residuals[c, place(me), :] = residuals[c, place(me), :] - arrived[k, c]
            return carry

        lax.fori_loop(0, sec, subtract, 0)
        spread(residuals, 0, c)

    @pl.when(sec == 0)
    def _():
        begin(0)

    prepare(0, 0)
    lax.fori_loop(sec + 1, sections, prepare, 0)

    def advance(c, carry):
        @pl.when(sec > 0)
        def _():
            begin(c)

        relay(residuals, 0, c)

        @pl.when(jnp.logical_and(sec == 0, c + 1 < micro))
        def _():
            begin(c + 1)

        finish(residuals, 0, c)
        result = multiply(0)
        solved[c, place(me), :] = result
        out[:, pl.ds(pl.multiple_of(c * width, width), width)] = result

        @pl.when(sec + 1 < sections)
        def _():
            spread(solved, 1, c)
            relay(solved, 1, c)
            finish(solved, 1, c)

            def send(i, carry):
                leaving[i, c] = multiply(i)
                part_copy(sec, i, c).start()
                return carry

            lax.fori_loop(sec + 1, sections, send, 0)

        return carry

    lax.fori_loop(0, micro, advance, 0)

    def drain(c, carry):
        def sent(buffer, kind):
            for number in range(group - 1):
                copy_of(buffer, kind, c, me, number, me).wait_send()

        sent(residuals, 0)

        @pl.when(sec + 1 < sections)
        def _():
            sent(solved, 1)

            def wait_part(i, carry):
                part_copy(sec, i, c).wait_send()
                return carry

            lax.fori_loop(sec + 1, sections, wait_part, 0)

        return carry

    lax.fori_loop(0, micro, drain, 0)


def solution(mesh):
    sections, group = mesh.shape["sec"], mesh.shape["row"]
    columns = max(1, sections // 2)
    while group % columns:
        columns -= 1
    lines = group // columns

    def shards(factor, inverse_blocks, right_side):
        rows, depth = factor.shape[1], factor.shape[2]
        total = right_side.shape[2]
        micro = total // WIDTH
        bf16, f32 = jnp.bfloat16, jnp.float32
        result = pl.pallas_call(
            functools.partial(kernel, sections, lines, columns, micro),
            out_shape=jax.ShapeDtypeStruct((rows, total), f32),
            in_specs=[
                pl.BlockSpec(memory_space=pl.ANY),
                pl.BlockSpec(memory_space=pl.ANY),
                pl.BlockSpec(memory_space=pltpu.VMEM),
            ],
            out_specs=pl.BlockSpec(memory_space=pltpu.VMEM),
            scratch_shapes=[
                pltpu.VMEM((sections, rows, depth), f32),
                pltpu.VMEM((sections, 2 * rows, depth), bf16),
                pltpu.VMEM((micro, depth, WIDTH), f32),
                pltpu.VMEM((micro, depth, WIDTH), f32),
                pltpu.VMEM((depth, 2 * WIDTH), bf16),
                pltpu.VMEM((2 * rows, 2 * WIDTH), f32),
                pltpu.VMEM((sections, micro, rows, WIDTH), f32),
                pltpu.VMEM((sections, micro, rows, WIDTH), f32),
                pltpu.SemaphoreType.DMA((sections,)),
                pltpu.SemaphoreType.DMA((2, micro, group)),
                pltpu.SemaphoreType.DMA((2, micro, group)),
                pltpu.SemaphoreType.DMA((sections, micro)),
                pltpu.SemaphoreType.DMA((sections, micro)),
            ],
            compiler_params=pltpu.CompilerParams(
                collective_id=0, has_side_effects=True, vmem_limit_bytes=56 * 2**20
            ),
        )(factor, inverse_blocks[0], right_side[0])
        return result[None]

    return jax.shard_map(
        shards,
        mesh=mesh,
        in_specs=(P(None, "row", "sec"), P("sec", "row", None), P("sec", "row", None)),
        out_specs=P("sec", "row", None),
        check_vma=False,
    )
```

time: 666 us -> 181 us (0.27)
  waiting for transfers between devices: 517 us -> 0 us
  Pallas kernels: 0 us -> 179 us
  matrix products: 97.1 us -> 0 us
  starting transfers between devices: 15.8 us -> 0 us
  between operations: 13.4 us -> 0.01 us
  local copies, waits for them, and re-layouts: 11.1 us -> 1.77 us
    all_gather x12 -> x0, waiting for transfers between devices: 497 us -> none  [the longest x6 267 us: advance(): full_residual = lax.all_gather(residual, 'row', axis=0, tiled=True)]
    pallas_call x0 -> x1, Pallas kernels: none -> 179 us  [shards(): pl.pallas_call(functools.partial(kernel, sections, lines, columns, micro)...]
    dot_general x12 -> x0, matrix products: 97.1 us -> none  [the longest x6 68.4 us: fold_update(): return carry + jnp.dot(panel_rows, piece, precision=highest)]
    ppermute x12 -> x0, waiting for transfers between devices: 19.5 us -> none  [passed_along(): return lax.ppermute(block, axis, route)]
    ppermute x12 -> x0, starting transfers between devices: 15.5 us -> none  [passed_along(): return lax.ppermute(block, axis, route)]
    dynamic_slice x18 -> x0, local copies, waits for them, and re-layouts: 6.77 us -> none  [the longest x12 6.06 us: advance(): own_rhs = lax.dynamic_slice_in_dim(right_side[0], start_col, width, 1)]
  transfers between devices with their start and end apart: 24 -> 0, of which waited for: 18 -> 0; matrix products, arithmetic and copies ran while one was open for 0% -> 0% of each run, Pallas kernels for 0% -> 0%
where the time goes in v1:
time: 181 us
  Pallas kernels  179 us (99%)
    pallas_call x1, Pallas kernels, shards(): pl.pallas_call(functools.partial(kernel, sections, lines, columns, micro)...  179 us

profile of v1, /device:TPU:3, one launch (start us, length us, event | category | flops | bytes accessed | tf_op | source)
XLA Modules:
  0.0 180.9 jit_solution(9943468434419865023)
XLA Ops:
  0.0 179.1 %shard_map.37 = f32[256,384]{1,0:T(8,128)} custom-call(f32[4,256,2048]{2,1,0:T(8,128)} %factor.1, f32[256,2048]{1,0:T(8,128)} %bitcast.3, f32[256,384]{1,0:T(8,128)} %bitcast.5), custom_call_target="tpu_custom_call" | custom-call | tf_op jit(solution)/shard_map/pallas_call | solution.py:210
  179.1 1.8 copy.5

commit v2 on v1

v2 whole, which is shorter than its diff:
```python
import functools

import jax
import jax.numpy as jnp
from jax import lax
from jax.experimental import pallas as pl
from jax.experimental.pallas import tpu as pltpu
from jax.sharding import PartitionSpec as P

MESH = pl.DeviceIdType.MESH
WIDTH = 128
PIECES = 2


def split(value):
    high = value.astype(jnp.bfloat16)
    low = (value - high.astype(jnp.float32)).astype(jnp.bfloat16)
    return high, low


def kernel(
    sections, lines, columns, micro, pieces,
    factor, inverse, rhs, out,
    staged, panels, residuals, solved, operand, product, arrived, leaving,
    following, load_sem, send_sem, recv_sem, part_send, part_recv, hand_sem, rhs_sem,
):
    width = WIDTH
    rows = rhs.shape[0]
    group = lines * columns
    sec = lax.axis_index("sec")
    me = lax.axis_index("row")
    z, y = me // columns, me % columns
    z_steps = [s for d in range(1, lines) for s in ([d] if 2 * d == lines else [d, lines - d]) if 2 * d <= lines]
    z_peers = [lax.rem(z + s, lines) * columns + y for s in z_steps]
    y_peers = [z * columns + lax.rem(y + s, columns) for s in range(1, columns)]
    lines_of = [lax.rem(z + s, lines) for s in z_steps]

    def load(slot, source):
        return pltpu.make_async_copy(source, staged.at[slot], load_sem.at[slot])

    load(0, inverse).start()

    def start_load(i, carry):
        load(i, factor.at[i]).start()
        return carry

    lax.fori_loop(sec + 1, sections, start_load, 0)

    barrier = pltpu.get_barrier_semaphore()
    for peer in z_peers + y_peers:
        for s in (0, 1, sections - 1):
            pl.semaphore_signal(barrier, inc=1, device_id=(lax.rem(sec + s, sections), peer), device_id_type=MESH)
    for s in range(1, sections):
        pl.semaphore_signal(barrier, inc=1, device_id=(lax.rem(sec + s, sections), me), device_id_type=MESH)
    pl.semaphore_wait(barrier, 3 * (len(z_peers) + len(y_peers)) + sections - 1)

    def prepare(slot, carry):
        load(slot, factor.at[slot]).wait()
        step = 64 if rows % 64 == 0 else rows

        def part(j, carry):
            at = pl.multiple_of(j * step, step)
            high, low = split(staged[slot, pl.ds(at, step), :])
            panels[slot, pl.ds(at, step), :] = high
            panels[slot, pl.ds(pl.multiple_of(rows + at, step), step), :] = low
            return carry

        return lax.fori_loop(0, rows // step, part, carry)

    def place(source):
        return pl.ds(pl.multiple_of(source * rows, rows), rows)

    length = rows // pieces

    def part_of(source, piece):
        return pl.ds(pl.multiple_of(source * rows + piece * length, length), length)

    def copy_of(buffer, kind, c, source, piece, number, peer):
        return pltpu.make_async_remote_copy(
            src_ref=buffer.at[c, part_of(source, piece), :],
            dst_ref=buffer.at[c, part_of(source, piece), :],
            send_sem=send_sem.at[kind, c, number, piece],
            recv_sem=recv_sem.at[kind, c, source, piece],
            device_id=(sec, peer),
            device_id_type=MESH,
        )

    def spread(buffer, kind, c):
        for piece in range(pieces):
            for number, peer in enumerate(z_peers + y_peers):
                copy_of(buffer, kind, c, me, piece, number, peer).start()

    def digest(buffer, kind, c, source):
        high, low = split(buffer[c, place(source), :])
        operand[kind, place(source), pl.ds(0, width)] = high
        operand[kind, place(source), pl.ds(width, width)] = low

    def relay(buffer, kind, c):
        for piece in range(pieces):
            number = len(z_peers) + len(y_peers)
            for peer in z_peers:
                copy_of(buffer, kind, c, peer, piece, 0, me).wait_recv()
                for target in y_peers:
                    copy_of(buffer, kind, c, peer, piece, number, target).start()
                    number += 1
        for peer in z_peers:
            digest(buffer, kind, c, peer)

    def arrive(buffer, kind, c, source):
        for piece in range(pieces):
            copy_of(buffer, kind, c, source, piece, 0, me).wait_recv()
        digest(buffer, kind, c, source)

    def finish(buffer, kind, c):
        for s in range(1, columns):
            column = lax.rem(y + s, columns)
            for line in [z] + lines_of:
                arrive(buffer, kind, c, line * columns + column)

    def multiply(slot, kind):
        product[...] = jnp.dot(panels[slot], operand[kind], preferred_element_type=jnp.float32)
        upper = product[pl.ds(0, rows), pl.ds(0, width)] + product[pl.ds(0, rows), pl.ds(width, width)]
        lower = product[pl.ds(rows, rows), pl.ds(0, width)] + product[pl.ds(rows, rows), pl.ds(width, width)]
        return upper + lower

    def far_copy(source, target, c):
        return pltpu.make_async_remote_copy(
            src_ref=leaving.at[target, c],
            dst_ref=arrived.at[source, c],
            send_sem=part_send.at[target, c],
            recv_sem=part_recv.at[source, c],
            device_id=(target - 1, me),
            device_id_type=MESH,
        )

    def cols_of(c):
        return pl.ds(pl.multiple_of(c * width, width), width)

    def begin(c):
        residuals[c, place(me), :] = rhs[:, cols_of(c)]
        spread(residuals, 0, c)
        digest(residuals, 0, c, me)

    def hand_copy(c, piece, number, peer):
        return pltpu.make_async_remote_copy(
            src_ref=leaving.at[0, c, pl.ds(piece * length, length), :],
            dst_ref=residuals.at[c, part_of(me, piece), :],
            send_sem=hand_sem.at[c, number, piece],
            recv_sem=recv_sem.at[0, c, me, piece],
            device_id=(sec + 1, peer),
            device_id_type=MESH,
        )

    def hand_on(c):
        leaving[0, c] = following[:, cols_of(c)] - multiply(sec + 1, 1)

        def subtract(k, carry):
            far_copy(k, sec + 1, c).wait_recv()
            leaving[0, c] = leaving[0, c] - arrived[k, c]
            return carry

        lax.fori_loop(0, sec, subtract, 0)
        for piece in range(pieces):
            for number, peer in enumerate(z_peers + y_peers + [me]):
                hand_copy(c, piece, number, peer).start()

    def rhs_copy():
        return pltpu.make_async_remote_copy(
            src_ref=rhs, dst_ref=following, send_sem=rhs_sem.at[0], recv_sem=rhs_sem.at[1],
            device_id=(sec - 1, me), device_id_type=MESH,
        )

    last = sec + 1 == sections

    @pl.when(sec == 0)
    def _():
        begin(0)

    @pl.when(sec > 0)
    def _():
        rhs_copy().start()

    prepare(0, 0)

    @pl.when(sec > 0)
    def _():
        lax.fori_loop(sec + 1, sections, prepare, 0)

    relay(residuals, 0, 0)

    def send(i, c):
        leaving[i, c] = multiply(i, 1)
        far_copy(sec, i, c).start()
        return c

    def advance(c, carry):
        more = c + 1 < micro

        @pl.when(sec > 0)
        def _():
            arrive(residuals, 0, c, me)

        finish(residuals, 0, c)
        result = multiply(0, 0)
        solved[c, place(me), :] = result

        @pl.when(jnp.logical_not(last))
        def _():
            spread(solved, 1, c)
            digest(solved, 1, c, me)

        out[:, cols_of(c)] = result

        @pl.when(jnp.logical_and(sec == 0, more))
        def _():
            begin(c + 1)

        @pl.when(jnp.logical_and(sec == 0, c == 0))
        def _():
            lax.fori_loop(1, sections, prepare, 0)

        @pl.when(jnp.logical_not(last))
        def _():
            @pl.when(c == 0)
            def _():
                pltpu.make_async_remote_copy(
                    src_ref=rhs, dst_ref=following, send_sem=rhs_sem.at[0], recv_sem=rhs_sem.at[1],
                    device_id=(sec, me), device_id_type=MESH,
                ).wait_recv()

            relay(solved, 1, c)
            @pl.when(more)
            def _():
                relay(residuals, 0, c + 1)

            finish(solved, 1, c)
            hand_on(c)

        @pl.when(jnp.logical_and(last, more))
        def _():
            relay(residuals, 0, c + 1)

        lax.fori_loop(sec + 2, sections, send, c)
        return carry

    lax.fori_loop(0, micro, advance, 0)

    def drain(c, carry):
        for piece in range(pieces):
            for number in range(group - 1):
                own = len(z_peers) + len(y_peers)

                def sent():
                    copy_of(residuals, 0, c, me, piece, number, me).wait_send()

                if number >= own:
                    sent()
                else:
                    pl.when(sec == 0)(sent)

            @pl.when(jnp.logical_not(last))
            def _():
                for number in range(group - 1):
                    copy_of(solved, 1, c, me, piece, number, me).wait_send()
                for number in range(len(z_peers) + len(y_peers) + 1):
                    hand_copy(c, piece, number, me).wait_send()

        def wait_far(i, carry):
            far_copy(sec, i, c).wait_send()
            return carry

        lax.fori_loop(sec + 2, sections, wait_far, 0)
        return carry

    lax.fori_loop(0, micro, drain, 0)

    @pl.when(sec > 0)
    def _():
        rhs_copy().wait_send()


def solution(mesh):
    sections, group = mesh.shape["sec"], mesh.shape["row"]
    columns = max(1, sections // 2)
    while group % columns:
        columns -= 1
    lines = group // columns

    def shards(factor, inverse_blocks, right_side):
        rows, depth = factor.shape[1], factor.shape[2]
        total = right_side.shape[2]
        micro = total // WIDTH
        pieces = PIECES if rows % (8 * PIECES) == 0 else 1
        bf16, f32 = jnp.bfloat16, jnp.float32
        result = pl.pallas_call(
            functools.partial(kernel, sections, lines, columns, micro, pieces),
            out_shape=jax.ShapeDtypeStruct((rows, total), f32),
            in_specs=[
                pl.BlockSpec(memory_space=pl.ANY),
                pl.BlockSpec(memory_space=pl.ANY),
                pl.BlockSpec(memory_space=pltpu.VMEM),
            ],
            out_specs=pl.BlockSpec(memory_space=pltpu.VMEM),
            scratch_shapes=[
                pltpu.VMEM((sections, rows, depth), f32),
                pltpu.VMEM((sections, 2 * rows, depth), bf16),
                pltpu.VMEM((micro, depth, WIDTH), f32),
                pltpu.VMEM((micro, depth, WIDTH), f32),
                pltpu.VMEM((2, depth, 2 * WIDTH), bf16),
                pltpu.VMEM((2 * rows, 2 * WIDTH), f32),
                pltpu.VMEM((sections, micro, rows, WIDTH), f32),
                pltpu.VMEM((sections, micro, rows, WIDTH), f32),
                pltpu.VMEM((rows, total), f32),
                pltpu.SemaphoreType.DMA((sections,)),
                pltpu.SemaphoreType.DMA((2, micro, group, pieces)),
                pltpu.SemaphoreType.DMA((2, micro, group, pieces)),
                pltpu.SemaphoreType.DMA((sections, micro)),
                pltpu.SemaphoreType.DMA((sections, micro)),
                pltpu.SemaphoreType.DMA((micro, lines + columns - 1, pieces)),
                pltpu.SemaphoreType.DMA((2,)),
            ],
            compiler_params=pltpu.CompilerParams(
                collective_id=0, has_side_effects=True, vmem_limit_bytes=56 * 2**20
            ),
        )(factor, inverse_blocks[0], right_side[0])
        return result[None]

    return jax.shard_map(
        shards,
        mesh=mesh,
        in_specs=(P(None, "row", "sec"), P("sec", "row", None), P("sec", "row", None)),
        out_specs=P("sec", "row", None),
        check_vma=False,
    )
```

time: 181 us -> 152 us (0.84)
  Pallas kernels: 179 us -> 150 us
    pallas_call x1, Pallas kernels: 179 us -> 150 us  [shards(): pl.pallas_call(functools.partial(kernel, sections, lines, columns, micro,...]
where the time goes in v2:
time: 152 us
  Pallas kernels  150 us (99%)
  local copies, waits for them, and re-layouts  1.77 us (1%)
    pallas_call x1, Pallas kernels, shards(): pl.pallas_call(functools.partial(kernel, sections, lines, columns, micro,...  150 us

profile of v2, /device:TPU:3, one launch (start us, length us, event | category | flops | bytes accessed | tf_op | source)
XLA Modules:
  0.0 151.6 jit_solution(8485851388708150586)
XLA Ops:
  0.0 149.8 %shard_map.37 = f32[256,384]{1,0:T(8,128)} custom-call(f32[4,256,2048]{2,1,0:T(8,128)} %factor.1, f32[256,2048]{1,0:T(8,128)} %bitcast.3, f32[256,384]{1,0:T(8,128)} %bitcast.5), custom_call_target="tpu_custom_call" | custom-call | tf_op jit(solution)/shard_map/pallas_call | solution.py:295
  149.8 1.8 %copy.5 = f32[1,256,384]{2,1,0:T(8,128)} copy(f32[1,256,384]{2,1,0:T(8,128)} %bitcast.4) | data formatting | bytes 786432

commit v3 on v2

--- a/solution.py
+++ b/solution.py
@@ -34,6 +34,15 @@
     z_peers = [lax.rem(z + s, lines) * columns + y for s in z_steps]
     y_peers = [z * columns + lax.rem(y + s, columns) for s in range(1, columns)]
     lines_of = [lax.rem(z + s, lines) for s in z_steps]
+    half = lines // 2 if lines % 2 == 0 else lines
+    side = z // half
+    mates = [(side * half + lax.rem(z + s, half)) * columns + y for s in range(1, half)]
+    gate = half - 1 + side
+    is_gate = z == gate
+    far_lines = [half - side + j * (1 - 2 * side) for j in range(half)] if half < lines else []
+    far = [line * columns + y for line in far_lines]
+    targets = mates + far[:1] + y_peers
+    relayed = (lines - 1) * (columns - 1)
 
     def load(slot, source):
         return pltpu.make_async_copy(source, staged.at[slot], load_sem.at[slot])
@@ -87,7 +96,7 @@
 
     def spread(buffer, kind, c):
         for piece in range(pieces):
-            for number, peer in enumerate(z_peers + y_peers):
+            for number, peer in enumerate(targets):
                 copy_of(buffer, kind, c, me, piece, number, peer).start()
 
     def digest(buffer, kind, c, source):
@@ -97,13 +106,21 @@
 
     def relay(buffer, kind, c):
         for piece in range(pieces):
-            number = len(z_peers) + len(y_peers)
-            for peer in z_peers:
+            number = len(targets)
+            inner = number + relayed
+            for peer in mates + far:
                 copy_of(buffer, kind, c, peer, piece, 0, me).wait_recv()
+                if any(peer is source for source in far) and mates:
+                    def pass_on(peer=peer, inner=inner):
+                        for step, mate in enumerate(mates):
+                            copy_of(buffer, kind, c, peer, piece, inner + step, mate).start()
+
+                    pl.when(is_gate)(pass_on)
+                    inner += len(mates)
                 for target in y_peers:
                     copy_of(buffer, kind, c, peer, piece, number, target).start()
                     number += 1
-        for peer in z_peers:
+        for peer in mates + far:
             digest(buffer, kind, c, peer)
 
     def arrive(buffer, kind, c, source):
@@ -161,7 +178,7 @@
 
         lax.fori_loop(0, sec, subtract, 0)
         for piece in range(pieces):
-            for number, peer in enumerate(z_peers + y_peers + [me]):
+            for number, peer in enumerate(targets + [me]):
                 hand_copy(c, piece, number, peer).start()
 
     def rhs_copy():
@@ -246,23 +263,35 @@
     lax.fori_loop(0, micro, advance, 0)
 
     def drain(c, carry):
-        for piece in range(pieces):
-            for number in range(group - 1):
-                own = len(z_peers) + len(y_peers)
-
-                def sent():
-                    copy_of(residuals, 0, c, me, piece, number, me).wait_send()
-
-                if number >= own:
-                    sent()
-                else:
-                    pl.when(sec == 0)(sent)
-
-            @pl.when(jnp.logical_not(last))
+        def sent(buffer, kind, numbers):
+            for piece in range(pieces):
+                for number in numbers:
+                    copy_of(buffer, kind, c, me, piece, number, me).wait_send()
+
+        own = range(len(targets))
+        across = range(len(targets), len(targets) + relayed)
+        inside = range(len(targets) + relayed, len(targets) + relayed + len(far) * len(mates))
+        sent(residuals, 0, across)
+
+        @pl.when(sec == 0)
+        def _():
+            sent(residuals, 0, own)
+
+        @pl.when(is_gate)
+        def _():
+            sent(residuals, 0, inside)
+
+        @pl.when(jnp.logical_not(last))
+        def _():
+            sent(solved, 1, own)
+            sent(solved, 1, across)
+
+            @pl.when(is_gate)
             def _():
-                for number in range(group - 1):
-                    copy_of(solved, 1, c, me, piece, number, me).wait_send()
-                for number in range(len(z_peers) + len(y_peers) + 1):
+                sent(solved, 1, inside)
+
+            for piece in range(pieces):
+                for number in range(len(targets) + 1):
                     hand_copy(c, piece, number, me).wait_send()
 
         def wait_far(i, carry):
@@ -291,6 +320,8 @@
         total = right_side.shape[2]
         micro = total // WIDTH
         pieces = PIECES if rows % (8 * PIECES) == 0 else 1
+        half = lines // 2 if lines % 2 == 0 else lines
+        numbers = half + columns - 1 + (lines - 1) * (columns - 1) + half * (half - 1)
         bf16, f32 = jnp.bfloat16, jnp.float32
         result = pl.pallas_call(
             functools.partial(kernel, sections, lines, columns, micro, pieces),
@@ -312,7 +343,7 @@
                 pltpu.VMEM((sections, micro, rows, WIDTH), f32),
                 pltpu.VMEM((rows, total), f32),
                 pltpu.SemaphoreType.DMA((sections,)),
-                pltpu.SemaphoreType.DMA((2, micro, group, pieces)),
+                pltpu.SemaphoreType.DMA((2, micro, numbers, pieces)),
                 pltpu.SemaphoreType.DMA((2, micro, group, pieces)),
                 pltpu.SemaphoreType.DMA((sections, micro)),
                 pltpu.SemaphoreType.DMA((sections, micro)),

time: 152 us -> 147 us (0.967)
  Pallas kernels: 150 us -> 145 us
    pallas_call x1, Pallas kernels: 150 us -> 145 us  [shards(): pl.pallas_call(functools.partial(kernel, sections, lines, columns, micro,...]
where the time goes in v3:
time: 147 us
  Pallas kernels  145 us (99%)
  local copies, waits for them, and re-layouts  1.77 us (1%)
    pallas_call x1, Pallas kernels, shards(): pl.pallas_call(functools.partial(kernel, sections, lines, columns, micro,...  145 us

profile of v3, /device:TPU:3, one launch (start us, length us, event | category | flops | bytes accessed | tf_op | source)
XLA Modules:
  0.0 147.2 jit_solution(16111083957900773591)
XLA Ops:
  0.0 145.5 %shard_map.37 = f32[256,384]{1,0:T(8,128)} custom-call(f32[4,256,2048]{2,1,0:T(8,128)} %factor.1, f32[256,2048]{1,0:T(8,128)} %bitcast.3, f32[256,384]{1,0:T(8,128)} %bitcast.5), custom_call_target="tpu_custom_call" | custom-call | tf_op jit(solution)/shard_map/pallas_call | solution.py:326
  145.5 1.8 %copy.5 = f32[1,256,384]{2,1,0:T(8,128)} copy(f32[1,256,384]{2,1,0:T(8,128)} %bitcast.4) | data formatting | bytes 786432
